TPU v7x, 32 devices: a whole 2x2x4 slice. The times are simulated.
32 devices in a mesh: wafer: 2 (over x), die: 16 (over z, y, core).
Axes of the slice: x: 2, y: 2, z: 4, core: 2. Of those that a mesh axis runs over, the one named last changes fastest.
Arguments:
- die_tiles: float32 [512, 64, 1024], P(('wafer', 'die')), parts along dimension 0, may hold values from -14 to 14
- slot_pos: int32 [512], P(('wafer', 'die')), parts along dimension 0, may hold values from 0 to 31, as said below
- slot_die: int32 [512], P(('wafer', 'die')), parts along dimension 0, may hold values from 0 to 7
- present: int32 [16, 32], P('wafer'), parts along dimension 0, may hold values from 0 to 1, as said below
- strength: float32 [32, 64, 1024], P('die'), may hold values from 0.3 to 3
- kernel: float32 [5, 5], replicated, may hold values from 0.1 to 1
Outputs:
- residual: float32 [512, 64, 1024], P(('wafer', 'die')), parts along dimension 0
There are 2 independent parts, one for each index of `wafer`. A program takes and returns all parts, laid end to end along the dimension named above; an argument that names none is the same for every part. Nothing has to cross between parts.
Inputs may be any that keep to these rules, and one draw needn't show every extreme that they name: `slot_pos`: each pair of position and die stands in exactly one slot. Among the slots of one device, at most 2 hold positions with equal position // 2, and this most is reached on every device; every value of position // 2 is held by 16 slots in all. At every position at least 6 dies are present.
All inputs are finite; a program needn't handle non-finite values.
Results may differ from a plain program's by a relative error of at most 0.0001.
Values sent between devices are 32-bit elements; how exact they have to be, the bound alone decides.
A program may use at most 128 MiB of HBM per device.

v0:
```python
import jax
import jax.numpy as jnp
from jax import lax
from jax.sharding import PartitionSpec as P

POS_DEV = 2
CAP = 2
ITERS = 3


def smooth(extended, field, strength, kernel, cols):
    length = field.shape[1]
    padded = jnp.pad(extended, ((0, 0), (2, 2)))
    column = jnp.arange(length, dtype=jnp.int32) % cols
    total = jnp.zeros_like(field)
    for shift_row in range(5):
        for shift_col in range(5):
            inside = (column + shift_col - 2 >= 0) & (column + shift_col - 2 < cols)
            start = shift_row * cols + shift_col
            shifted = padded[:, start : start + length]
            total = total + kernel[shift_row, shift_col] * jnp.where(inside[None, :], shifted, 0.0)
    return (field + strength * total) / (1.0 + strength * jnp.sum(kernel))


def huber_passes(stack, live, strength, kernel, extend, cols):
    weight0 = live[:, :, None]
    mean = jnp.sum(weight0 * stack, axis=1) / jnp.sum(live, axis=1)[:, None]
    refer = mean
    for step in range(ITERS):
        gap = jnp.abs(stack - refer[:, None])
        weight = weight0 * 1.5 / jnp.maximum(gap, 1.5)
        mean = jnp.sum(weight * stack, axis=1) / jnp.sum(weight, axis=1)
        refer = smooth(extend(mean), mean, strength, kernel, cols)
    return refer


def presence(dies_of, places_of, present):
    dies = present.shape[0]
    places = present.shape[1]
    die_hit = dies_of[:, None] == jnp.arange(dies, dtype=jnp.int32)[None, :]
    place_hit = places_of[:, None] == jnp.arange(places, dtype=jnp.int32)[None, :]
    table = die_hit[:, :, None] & place_hit[:, None, :] & (present[None] == 1)
    return jnp.any(table, axis=(1, 2)).astype(jnp.float32)


def shards(die_tiles, slot_pos, slot_die, present, strength, kernel):
    group = lax.axis_size("die")
    myself = lax.axis_index("die")
    slots = die_tiles.shape[0]
    rows = die_tiles.shape[1]
    cols = die_tiles.shape[2]
    dies = present.shape[0]
    all_pos, all_die = (
        lax.all_gather(slot_pos, "die", axis=0, tiled=True),
        lax.all_gather(slot_die, "die", axis=0, tiled=True),
    )
    pos_grid = all_pos.reshape(group, slots)
    die_grid = all_die.reshape(group, slots)
    owners = pos_grid // POS_DEV
    order = jnp.arange(slots, dtype=jnp.int32)
    earlier = order[None, :] < order[:, None]
    same = owners[:, :, None] == owners[:, None, :]
    rank = jnp.sum((same & earlier[None]).astype(jnp.int32), axis=2)
    bucket = owners * CAP + rank
    mine = lax.dynamic_index_in_dim(bucket, myself, 0, keepdims=False)
    buckets = group * CAP
    match = mine[None, :] == jnp.arange(buckets, dtype=jnp.int32)[:, None]
    source_slot = jnp.sum(jnp.where(match, order[None, :], 0), axis=1)
    filled = jnp.any(match, axis=1)
    outgoing = jnp.where(filled[:, None, None], die_tiles[source_slot], 0.0).reshape(
        group, CAP, rows, cols
    )
    arrived = lax.all_to_all(outgoing, "die", split_axis=0, concat_axis=0, tiled=True).reshape(
        buckets, rows * cols
    )
    entry = jnp.arange(group, dtype=jnp.int32)[:, None] * CAP + rank
    local_place = pos_grid - myself * POS_DEV
    local_pair = local_place * dies + die_grid
    toward = owners == myself
    targets = jnp.arange(POS_DEV * dies, dtype=jnp.int32)
    hit = toward[:, :, None] & (local_pair[:, :, None] == targets[None, None, :])
    chosen = jnp.sum(jnp.where(hit, entry[:, :, None], 0), axis=(0, 1))
    stack = arrived[chosen].reshape(POS_DEV, dies, rows * cols)
    live = lax.dynamic_slice_in_dim(present, myself * POS_DEV, POS_DEV, 1).T.astype(jnp.float32)

    def pad_rows(field):
        return jnp.pad(field, ((0, 0), (2 * cols, 2 * cols)))

    flat_strength = strength.reshape(POS_DEV, rows * cols)
    refer = huber_passes(stack, live, flat_strength, kernel, pad_rows, cols)
    entries = jnp.arange(buckets, dtype=jnp.int32)
    hit_entry = toward[:, :, None] & (entry[:, :, None] == entries[None, None, :])
    entry_place = jnp.sum(jnp.where(hit_entry, local_place[:, :, None], 0), axis=(0, 1))
    returning = refer[entry_place].reshape(group, CAP, rows, cols)
    back = lax.all_to_all(returning, "die", split_axis=0, concat_axis=0, tiled=True).reshape(
        buckets, rows, cols
    )
    keep = presence(slot_die, slot_pos, present)
    return keep[:, None, None] * (die_tiles - back[mine])


def solution(mesh):
    placed = (
        P(("wafer", "die"), None, None),
        P(("wafer", "die")),
        P(("wafer", "die")),
        P("wafer", None),
        P("die", None, None),
        P(),
    )
    return jax.shard_map(
        shards,
        mesh=mesh,
        in_specs=placed,
        out_specs=P(("wafer", "die"), None, None),
        check_vma=False,
    )
```

profile of v0, /device:TPU:13, one launch (start us, length us, event | category | flops | bytes accessed | tf_op | source)
XLA Modules:
  0.0 558.5 jit_solution(156588044128892569)
XLA Ops:
  0.0 1.2 dynamic-slice
  1.9 0.9 dynamic-update-slice
  2.8 0.8 dynamic-update-slice.1
  3.6 7.9 %all-reduce.8 = (s32[256]{0:T(256)S(1)}, s32[256]{0:T(256)S(1)}) all-reduce(s32[256]{0:T(256)S(1)} %dynamic-update-slice, s32[256]{0:T(256)S(1)} %dynamic-update-slice.1), channel_id=1, replica_groups=mesh['wafer'=2,'die'=16] {'die'}, use_global_device_ids=true, to_apply=%add.6 | all-reduce | flops 512 | bytes 4096
  11.5 0.1 reshape.306
  11.6 0.4 convert_reduce_fusion
  12.1 0.1 select_reduce_fusion.2
  12.2 0.1 fusion.42
  12.2 0.1 reshape.308
  12.3 0.1 broadcast_add_fusion
  12.4 0.2 select_reduce_fusion
  12.6 0.1 broadcast_in_dim.616
  12.7 6.5 %gather_fusion = f32[32,64,1024]{2,1,0:T(8,128)} fusion(f32[16,64,1024]{2,1,0:T(8,128)} %param.6, s32[1024]{0:T(1024)S(1)} %pad_clamp_fusion.3), kind=kCustom, calls=%fused_computation | custom fusion | bytes 16777344 | tf_op jit(solution)/shard_map/gather | solution.py:70
  19.2 8.7 %broadcast_select_fusion = f32[16,2,64,1024]{3,2,1,0:T(8,128)} fusion(f32[16,2,64,1024]{3,2,1,0:T(8,128)} %bitcast.103, pred[16,2]{1,0:T(8,128)(4,1)S(1)} %broadcast_in_dim.616), kind=kLoop, calls=%fused_computation.25 | loop fusion | flops 2097152 | bytes 16777248 | tf_op jit(solution)/shard_map/jit(_where)/select_n | solution.py:70
  27.9 0.0 copy-start.3
  27.9 0.0 copy-start.1
  27.9 0.0 copy-start.2
  27.9 9.9 %all-to-all-start = ((f32[16,2,64,1024]{3,2,1,0:T(8,128)}), f32[16,2,64,1024]{3,2,1,0:T(8,128)}, u32[]{:S(2)}, u32[]{:S(2)}) async-start(f32[16,2,64,1024]{3,2,1,0:T(8,128)} %broadcast_select_fusion), calls=%async_computation | async-start | bytes 16777216 | tf_op jit(solution)/shard_map/all_to_all | solution.py:73
  37.8 0.0 copy-done.3
  37.8 0.1 convert_reduce_fusion.1
  37.9 0.1 broadcast_multiply_fusion
  37.9 0.1 copy.12
  38.0 0.1 copy.11
  38.1 0.0 copy-done.1
  38.1 0.4 copy.14
  38.5 0.0 copy-done.2
  38.5 0.6 reduce_sum.140
  39.1 0.2 select_reduce_fusion.1
  39.3 0.7 fusion.52
  40.0 0.7 fusion.51
  40.8 0.1 fusion.33
  40.9 0.1 fusion.35
  41.0 178.9 %all-to-all-done = f32[16,2,64,1024]{3,2,1,0:T(8,128)} async-done(((f32[16,2,64,1024]{3,2,1,0:T(8,128)}), f32[16,2,64,1024]{3,2,1,0:T(8,128)}, u32[]{:S(2)}, u32[]{:S(2)}) %all-to-all-start) | async-done | bytes 8388640 | tf_op jit(solution)/shard_map/all_to_all | solution.py:73
  220.0 11.4 %copy.13 = f32[4,8,64,1024]{3,1,2,0:T(8,128)} copy(f32[4,8,64,1024]{3,2,1,0:T(8,128)} %bitcast.40) | data formatting | bytes 16777216
  231.4 8.8 %gather_fusion.1 = f32[16,65536]{1,0:T(8,128)} fusion(f32[32,65536]{1,0:T(8,128)} %bitcast.102, s32[1024]{0:T(1024)S(1)} %pad_clamp_fusion.2), kind=kCustom, calls=%fused_computation.1 | custom fusion | bytes 8388672 | tf_op jit(solution)/shard_map/gather | solution.py:83
  240.3 0.0 copy-start
  240.3 3.9 fusion
  244.2 0.2 broadcast_divide_fusion
  244.4 0.0 copy-done
  244.4 4.0 fusion.15
  248.4 0.3 div.67
  248.7 0.2 pad.20
  248.9 27.6 %fusion.16 = f32[2,65536]{1,0:T(2,128)S(1)} fusion(f32[2,65536]{1,0:T(2,128)S(1)} %bitcast.106, f32[2,65536]{1,0:T(2,128)S(1)} %div.67, f32[2,69632]{1,0:T(2,128)S(1)} %pad.20, pred[65536]{0:T(1024)(128)(4,1)S(1)} %get-tuple-element.48, pred[65536]{0:T(1024)(128)(4,1)S(1)} %get-tuple-element.49, pred[65536]{0:T(1024)(128)(4,1)S(1)} %fusion.37, ...), kind=kLoop, calls=%fused_computation.32 | loop fusion | flops 10354688 | bytes 12943464 | tf_op jit(solution)/shard_map/div | solution.py:22
  276.5 3.6 fusion.14
  280.1 0.3 div.70
  280.4 0.2 pad.22
  280.6 27.8 %add_divide_fusion.1 = f32[2,65536]{1,0:T(2,128)S(1)} fusion(f32[2,65536]{1,0:T(2,128)S(1)} %div.70, f32[2,65536]{1,0:T(2,128)S(1)} %bitcast.107, f32[2,69632]{1,0:T(2,128)S(1)} %pad.22, pred[65536]{0:T(1024)(128)(4,1)S(1)} %get-tuple-element.48, pred[65536]{0:T(1024)(128)(4,1)S(1)} %get-tuple-element.49, pred[65536]{0:T(1024)(128)(4,1)S(1)} %fusion.37, ...), kind=kLoop, calls=%fused_computation.30 | loop fusion | flops 10354688 | bytes 12943464 | tf_op jit(solution)/shard_map/div | solution.py:22
  308.4 3.6 fusion.13
  312.0 0.3 div.73
  312.2 0.2 pad.24
  312.4 27.6 %add_divide_fusion = f32[2,65536]{1,0:T(2,128)S(1)} fusion(f32[2,65536]{1,0:T(2,128)S(1)} %div.73, f32[2,65536]{1,0:T(2,128)S(1)} %bitcast.108, f32[2,69632]{1,0:T(2,128)S(1)} %pad.24, pred[65536]{0:T(1024)(128)(4,1)S(1)} %get-tuple-element.48, pred[65536]{0:T(1024)(128)(4,1)S(1)} %get-tuple-element.49, pred[65536]{0:T(1024)(128)(4,1)S(1)} %fusion.37, ...), kind=kLoop, calls=%fused_computation.29 | loop fusion | flops 10354688 | bytes 12943464 | tf_op jit(solution)/shard_map/div | solution.py:22
  340.1 6.2 %gather_fusion.2 = f32[32,65536]{1,0:T(8,128)} fusion(f32[2,65536]{1,0:T(2,128)S(1)} %add_divide_fusion, s32[1024]{0:T(1024)S(1)} %pad_clamp_fusion.1), kind=kCustom, calls=%fused_computation.2 | custom fusion | bytes 16777344 | tf_op jit(solution)/shard_map/gather | solution.py:94
  346.3 11.5 %copy.15 = f32[4,8,64,1024]{3,2,1,0:T(8,128)} copy(f32[4,8,64,1024]{3,1,2,0:T(8,128)} %bitcast.105) | data formatting | bytes 16777216
  357.7 0.0 copy-start.4
  357.7 0.0 copy-start.5
  357.7 5.0 all-to-all-start.1
  362.7 0.0 copy-done.4
  362.8 0.1 iota_compare_fusion.4
  362.8 0.0 copy-done.5
  362.8 0.1 iota_compare_fusion.5
  362.9 0.4 and_reduce_fusion
  363.4 181.7 %all-to-all-done.1 = f32[16,2,64,1024]{3,2,1,0:T(8,128)} async-done(((f32[16,2,64,1024]{3,2,1,0:T(8,128)}), f32[16,2,64,1024]{3,2,1,0:T(8,128)}, u32[]{:S(2)}, u32[]{:S(2)}) %all-to-all-start.1) | async-done | bytes 8388640 | tf_op jit(solution)/shard_map/all_to_all | solution.py:95
  545.1 6.2 %gather_fusion.3 = f32[16,64,1024]{2,1,0:T(8,128)} fusion(f32[32,64,1024]{2,1,0:T(8,128)} %bitcast.36, s32[1024]{0:T(1024)S(1)} %pad_clamp_fusion), kind=kCustom, calls=%fused_computation.3 | custom fusion | bytes 8388672 | tf_op jit(solution)/shard_map/gather | solution.py:99
  551.3 7.0 %subtract_multiply_fusion = f32[16,64,1024]{2,1,0:T(8,128)} fusion(f32[16,64,1024]{2,1,0:T(8,128)} %param.6, f32[16,64,1024]{2,1,0:T(8,128)} %gather_fusion.3, f32[16]{0:T(128)S(1)} %convert_element_type.24), kind=kLoop, calls=%fused_computation.24 | loop fusion | flops 2097152 | bytes 12582976 | tf_op jit(solution)/shard_map/mul | solution.py:99
  (16 shorter events, 0.1 us)
Async XLA Ops:
  27.9 9.9 %copy-start.3 = (s32[8,32]{1,0:T(8,128)S(1)}, s32[8,32]{1,0:T(8,128)}, u32[]{:S(2)}) copy-start(s32[8,32]{1,0:T(8,128)} %param.9) | copy-start | bytes 3076
  27.9 10.2 %copy-start.1 = (f32[2,64,1024]{2,1,0:T(8,128)S(1)}, f32[2,64,1024]{2,1,0:T(8,128)}, u32[]{:S(2)}) copy-start(f32[2,64,1024]{2,1,0:T(8,128)} %param.10) | copy-start | bytes 1572868
  27.9 10.7 %copy-start.2 = (f32[5,5]{1,0:T(8,128)S(1)}, f32[5,5]{1,0:T(8,128)}, u32[]{:S(2)}) copy-start(f32[5,5]{1,0:T(8,128)} %param.11) | copy-start | bytes 304
  27.9 192.1 %all-to-all-start = ((f32[16,2,64,1024]{3,2,1,0:T(8,128)}), f32[16,2,64,1024]{3,2,1,0:T(8,128)}, u32[]{:S(2)}, u32[]{:S(2)}) async-start(f32[16,2,64,1024]{3,2,1,0:T(8,128)} %broadcast_select_fusion), calls=%async_computation | async-start | bytes 16777216 | tf_op jit(solution)/shard_map/all_to_all | solution.py:73
  240.3 4.2 copy-start
  357.7 5.0 copy-start.4
  357.7 5.1 copy-start.5
  357.7 187.4 %all-to-all-start.1 = ((f32[16,2,64,1024]{3,2,1,0:T(8,128)}), f32[16,2,64,1024]{3,2,1,0:T(8,128)}, u32[]{:S(2)}, u32[]{:S(2)}) async-start(f32[16,2,64,1024]{3,2,1,0:T(8,128)} %bitcast.104), calls=%async_computation.1 | async-start | bytes 16777216 | tf_op jit(solution)/shard_map/all_to_all | solution.py:95
where the time goes:
time: 562 us; the launch traced here: 558 us
  waiting for transfers between devices  361 us (64%)
  other arithmetic  118 us (21%)
  local copies, waits for them, and re-layouts  56.4 us (10%)
  starting transfers between devices  14.9 us (3%)
  blocking collectives  7.89 us (1%)
    all_to_all x1, waiting for transfers between devices, shards(): lax.all_to_all(returning, 'die', split_axis=0, concat_axis=0, tiled=True)  182 us
    all_to_all x1, waiting for transfers between devices, shards(): lax.all_to_all(outgoing, 'die', split_axis=0, concat_axis=0, tiled=True)  179 us
    div x3, other arithmetic, smooth(): return (field + strength * total) / (1.0 + strength * jnp.sum(kernel))  83 us
    unnamed x20, local copies, waits for them, and re-layouts  26.3 us
  transfers between devices with their start and end apart: 2, of which 2 were waited for; matrix products, arithmetic and copies ran while one was open for 1% of the time, Pallas kernels for 0%

commit v1 on v0

v1 whole, which is shorter than its diff:
```python
import functools

import jax
import jax.numpy as jnp
from jax import lax
from jax.experimental import pallas as pl
from jax.experimental.pallas import tpu as pltpu
from jax.sharding import PartitionSpec as P

ITERS = 3
RS = 8
LANES = 128


def strip_of(q, strips):
    odd = q % 2
    half = q // 2
    return half * (1 - odd) + (strips - 1 - half) * odd


def chip_of(s, strips):
    high = s // (strips // 2)
    return 2 * s * (1 - high) + (2 * (strips - 1 - s) + 1) * high


def greet(n):
    me = lax.axis_index("die")
    barrier = pltpu.get_barrier_semaphore()
    for k in range(1, n):
        pl.semaphore_signal(barrier, inc=1, device_id={"die": (me + k) % n}, device_id_type=pl.DeviceIdType.MESH)
    pl.semaphore_wait(barrier, n - 1)


def remote(src, dst, send, recv, device):
    return pltpu.make_async_remote_copy(
        src_ref=src, dst_ref=dst, send_sem=send, recv_sem=recv,
        device_id={"die": device}, device_id_type=pl.DeviceIdType.MESH,
    )


def scatter_kernel(n, strips, blocks, cs, tiles, strength, arrived, power, send, recv, psend, precv, own):
    me = lax.axis_index("die")

    def region(device):
        s = strip_of(device // blocks, strips)
        c = device % blocks
        return pl.ds(pl.multiple_of(s * RS, RS), RS), pl.ds(pl.multiple_of(c * cs, LANES), cs)

    greet(n)
    copies = []
    for k in range(1, n):
        peer = (me + k) % n
        rows, cols = region(peer)
        copies.append(remote(tiles.at[:, rows, cols], arrived.at[me], send.at[k], recv.at[k], peer))
        copies[-1].start()
    for k in range(1, n):
        peer = (me + k) % n
        rows, cols = region(peer)
        copies.append(remote(strength.at[:, rows, cols], power.at[me], psend.at[k], precv.at[k], peer))
        copies[-1].start()
    rows, cols = region(me)
    copies.append(pltpu.make_async_copy(tiles.at[:, rows, cols], arrived.at[me], own.at[0]))
    copies[-1].start()
    copies.append(pltpu.make_async_copy(strength.at[:, rows, cols], power.at[me], own.at[1]))
    copies[-1].start()
    for copy in copies:
        copy.wait()


def refer_kernel(
    n, strips, blocks, cs, dies, positions,
    where, live, kern, arrived, power, out,
    stack, strength, mean, top, bottom, rows_up, rows_down, side_left, side_right, corners, ext, refer,
    load, hsend, hrecv, rsend, rrecv, ssend, srecv, own,
):
    me = lax.axis_index("die")
    s = strip_of(me // blocks, strips)
    c = me % blocks
    groups = positions // 4

    def device(ds, dc):
        return chip_of((s + ds + strips) % strips, strips) * blocks + (c + dc + blocks) % blocks

    loads = [
        pltpu.make_async_copy(arrived, stack, load.at[0]),
        pltpu.make_async_copy(power, strength, load.at[1]),
    ]
    for copy in loads:
        copy.start()
    greet(n)
    for copy in loads:
        copy.wait()

    first = pl.ds(0, LANES)
    last = pl.ds(cs - LANES, LANES)
    taps = [[kern[5 * a + b] for b in range(5)] for a in range(5)]
    total = taps[0][0]
    for a in range(5):
        for b in range(5):
            if a or b:
                total = total + taps[a][b]

    def exchange(k):
        copies = [
            remote(bottom.at[k], rows_up.at[k], hsend.at[k, 0], hrecv.at[k, 0], device(1, 0)),
            remote(top.at[k], rows_down.at[k], hsend.at[k, 1], hrecv.at[k, 1], device(-1, 0)),
            remote(mean.at[k, :, :, last], side_left.at[k], hsend.at[k, 2], hrecv.at[k, 2], device(0, 1)),
            remote(mean.at[k, :, :, first], side_right.at[k], hsend.at[k, 3], hrecv.at[k, 3], device(0, -1)),
            remote(bottom.at[k, :, :, last], corners.at[k, 0], hsend.at[k, 4], hrecv.at[k, 4], device(1, 1)),
            remote(bottom.at[k, :, :, first], corners.at[k, 1], hsend.at[k, 5], hrecv.at[k, 5], device(1, -1)),
            remote(top.at[k, :, :, last], corners.at[k, 2], hsend.at[k, 6], hrecv.at[k, 6], device(-1, 1)),
            remote(top.at[k, :, :, first], corners.at[k, 3], hsend.at[k, 7], hrecv.at[k, 7], device(-1, -1)),
        ]
        for copy in copies:
            copy.start()
        for copy in copies:
            copy.wait()

    def guard(flag, x):
        return jnp.where(flag, x, jnp.zeros_like(x))

    has_up, has_down, has_left, has_right = s > 0, s < strips - 1, c > 0, c < blocks - 1
    body = pl.ds(LANES, cs)
    right = pl.ds(LANES + cs, LANES)

    def smooth(k, g, j):
        p = 4 * g + j
        pair = pl.ds(2 * j, 2)
        field = mean[k, p]
        ext[j, 6:8, first] = guard(has_up & has_left, corners[k, 0, g, pair, :])
        ext[j, 6:8, body] = guard(has_up, rows_up[k, g, pair, :])
        ext[j, 6:8, right] = guard(has_up & has_right, corners[k, 1, g, pair, :])
        ext[j, 8:16, first] = guard(has_left, side_left[k, p])
        ext[j, 8:16, body] = field
        ext[j, 8:16, right] = guard(has_right, side_right[k, p])
        ext[j, 16:18, first] = guard(has_down & has_left, corners[k, 2, g, pair, :])
        ext[j, 16:18, body] = guard(has_down, rows_down[k, g, pair, :])
        ext[j, 16:18, right] = guard(has_down & has_right, corners[k, 3, g, pair, :])
        shifted = [ext[j, 6 + a : 14 + a, :] for a in range(5)]
        width = cs + 2 * LANES
        acc = None
        for b in range(5):
            part = shifted[0] * taps[0][b]
            for a in range(1, 5):
                part = part + shifted[a] * taps[a][b]
            if b != 2:
                part = pltpu.roll(part, (2 - b) % width, 1)
            part = part[:, LANES : LANES + cs]
            acc = part if acc is None else acc + part
        power_p = strength[p]
        return (field + power_p * acc) / (1.0 + power_p * total)

    def huber(k, g, j, ref):
        p = 4 * g + j
        num = None
        for d in range(dies):
            value = stack[where[p * dies + d]]
            weight = live[p * dies + d] / jnp.maximum(jnp.abs(value - ref), 1.5)
            num, den = (weight * value, weight) if num is None else (num + weight * value, den + weight)
        field = num / den
        mean[k, p] = field
        top[k, g, 2 * j : 2 * j + 2, :] = field[0:2]
        bottom[k, g, 2 * j : 2 * j + 2, :] = field[RS - 2 : RS]

    @pl.loop(0, groups)
    def _(g):
        for j in range(4):
            p = 4 * g + j
            count = live[p * dies]
            num = count * stack[where[p * dies]]
            for d in range(1, dies):
                share = live[p * dies + d]
                count = count + share
                num = num + share * stack[where[p * dies + d]]
            huber(0, g, j, num / jnp.full(num.shape, count))

    for k in range(1, ITERS):
        exchange(k - 1)

        @pl.loop(0, groups)
        def _(g):
            for j in range(4):
                huber(k, g, j, smooth(k - 1, g, j))

    exchange(ITERS - 1)

    @pl.loop(0, groups)
    def _(g):
        for j in range(4):
            refer[4 * g + j] = smooth(ITERS - 1, g, j)

    turn = 1 - 2 * (c % 2)
    ahead = device(turn, 0)
    mine = pltpu.make_async_copy(refer, out.at[s, c], own)
    mine.start()
    pending = []
    for t in range(strips):
        strip = (s - turn * t + strips) % strips
        block = refer if t == 0 else out.at[strip, c]
        if t:
            ring.wait_recv()
        if t < strips - 1:
            ring = remote(block, out.at[strip, c], rsend.at[t], rrecv.at[t], ahead)
            ring.start()
            pending.append(ring)
        for b in range(1, blocks):
            side = remote(block, out.at[strip, c], ssend.at[t, b], srecv.at[t, b], device(0, b))
            side.start()
            pending.append(side)
    for copy in pending:
        copy.wait_send()
    for t in range(strips):
        for b in range(1, blocks):
            source = (c - b + blocks) % blocks
            strip = (s - (1 - 2 * (source % 2)) * t + strips) % strips
            remote(out.at[strip, source], out.at[strip, source], ssend.at[t, b], srecv.at[t, b], device(0, b)).wait_recv()
    mine.wait()


def residual_kernel(strips, blocks, cs, pos, die, present, tile, refer, out):
    i = pl.program_id(0)
    keep = present[die[i], pos[i]].astype(jnp.float32)
    for s in range(strips):
        for c in range(blocks):
            rows, cols = pl.ds(s * RS, RS), pl.ds(c * cs, cs)
            out[0, rows, cols] = keep * (tile[0, rows, cols] - refer[s, c, 0])


def shards(n, die_tiles, slot_pos, slot_die, present, strength, kernel):
    slots, rows, cols = die_tiles.shape
    dies, positions = present.shape
    local = strength.shape[0]
    strips = rows // RS
    blocks = n // strips
    cs = cols // blocks
    hbm = pl.BlockSpec(memory_space=pl.ANY)
    smem = pl.BlockSpec(memory_space=pltpu.SMEM)
    dma = pltpu.SemaphoreType.DMA
    f32 = jnp.float32

    pair = slot_pos * dies + slot_die
    pairs = lax.all_gather(pair, "die", axis=0, tiled=True)
    count = positions * dies
    order = jnp.arange(n * slots, dtype=jnp.int32)
    where = jnp.sum(jnp.where(pairs[None, :] == jnp.arange(count, dtype=jnp.int32)[:, None], order[None, :], 0), axis=1)

    arrived, power = pl.pallas_call(
        functools.partial(scatter_kernel, n, strips, blocks, cs),
        name="scatter",
        out_shape=(
            jax.ShapeDtypeStruct((n, slots, RS, cs), f32),
            jax.ShapeDtypeStruct((n, local, RS, cs), f32),
        ),
        in_specs=[hbm, hbm],
        out_specs=(hbm, hbm),
        scratch_shapes=[dma((n,)), dma((n,)), dma((n,)), dma((n,)), dma((2,))],
        compiler_params=pltpu.CompilerParams(collective_id=0, has_side_effects=True),
    )(die_tiles, strength)

    groups = positions // 4
    vmem = pltpu.VMEM
    refer = pl.pallas_call(
        functools.partial(refer_kernel, n, strips, blocks, cs, dies, positions),
        name="refer",
        out_shape=jax.ShapeDtypeStruct((strips, blocks, positions, RS, cs), f32),
        in_specs=[smem, smem, smem, hbm, hbm],
        out_specs=hbm,
        scratch_shapes=[
            vmem((n * slots, RS, cs), f32),
            vmem((positions, RS, cs), f32),
            vmem((ITERS, positions, RS, cs), f32),
            vmem((ITERS, groups, 8, cs), f32),
            vmem((ITERS, groups, 8, cs), f32),
            vmem((ITERS, groups, 8, cs), f32),
            vmem((ITERS, groups, 8, cs), f32),
            vmem((ITERS, positions, RS, LANES), f32),
            vmem((ITERS, positions, RS, LANES), f32),
            vmem((ITERS, 4, groups, 8, LANES), f32),
            vmem((4, 24, cs + 2 * LANES), f32),
            vmem((positions, RS, cs), f32),
            dma((2,)),
            dma((ITERS, 8)),
            dma((ITERS, 8)),
            dma((strips,)),
            dma((strips,)),
            dma((strips, blocks)),
            dma((strips, blocks)),
            dma,
        ],
        compiler_params=pltpu.CompilerParams(
            collective_id=1, has_side_effects=True, vmem_limit_bytes=40 * 1024 * 1024
        ),
    )(
        where,
        present.T.astype(f32).reshape(count),
        kernel.reshape(25),
        arrived.reshape(n * slots, RS, cs),
        power.reshape(positions, RS, cs),
    )

    return pl.pallas_call(
        functools.partial(residual_kernel, strips, blocks, cs),
        name="residual",
        out_shape=jax.ShapeDtypeStruct((slots, rows, cols), f32),
        grid_spec=pltpu.PrefetchScalarGridSpec(
            num_scalar_prefetch=3,
            grid=(slots,),
            in_specs=[
                pl.BlockSpec((1, rows, cols), lambda i, *_: (i, 0, 0)),
                pl.BlockSpec((strips, blocks, 1, RS, cs), lambda i, pos, *_: (0, 0, pos[i], 0, 0)),
            ],
            out_specs=pl.BlockSpec((1, rows, cols), lambda i, *_: (i, 0, 0)),
        ),
    )(slot_pos, slot_die, present, die_tiles, refer)


def solution(mesh):
    placed = (
        P(("wafer", "die"), None, None),
        P(("wafer", "die")),
        P(("wafer", "die")),
        P("wafer", None),
        P("die", None, None),
        P(),
    )
    return jax.shard_map(
        functools.partial(shards, mesh.shape["die"]),
        mesh=mesh,
        in_specs=placed,
        out_specs=P(("wafer", "die"), None, None),
        check_vma=False,
    )
```

time: 562 us -> 239 us (0.43)
  waiting for transfers between devices: 361 us -> 0 us
  Pallas kernels: 0 us -> 217 us
  other arithmetic: 118 us -> 1.56 us
  local copies, waits for them, and re-layouts: 56.4 us -> 8.61 us
  starting transfers between devices: 14.9 us -> 0 us
    all_to_all x2 -> x0, waiting for transfers between devices: 361 us -> none  [the longest x1 182 us: shards(): lax.all_to_all(returning, 'die', split_axis=0, concat_axis=0, tiled=True)]
    pallas_call x0 -> x3, Pallas kernels: none -> 217 us  [the longest x1 110 us: shards(): pl.pallas_call(functools.partial(scatter_kernel, n, strips, blocks, cs),...]
    div x7 -> x0, other arithmetic: 84.1 us -> none  [the longest x3 83 us: smooth(): return (field + strength * total) / (1.0 + strength * jnp.sum(kernel))]
    gather x4 -> x0, local copies, waits for them, and re-layouts: 27.8 us -> none  [the longest x1 8.83 us: shards(): stack = arrived[chosen].reshape(POS_DEV, dies, rows * cols)]
    unnamed x20 -> x8, local copies, waits for them, and re-layouts: 26.3 us -> 7.67 us
    reduce_sum x10 -> x1, other arithmetic: 16.6 us -> 0.12 us  [shards(): jnp.sum(jnp.where(pairs[None, :] == jnp.arange(count, dtype=jnp.int32)[:,...]
    all_to_all x2 -> x0, starting transfers between devices: 14.9 us -> none  [the longest x1 9.89 us: shards(): lax.all_to_all(outgoing, 'die', split_axis=0, concat_axis=0, tiled=True)]
    select_n x4 -> x0, other arithmetic: 8.69 us -> none  [the longest x1 8.66 us: shards(): jnp.where(filled[:, None, None], die_tiles[source_slot], 0.0)]
  transfers between devices with their start and end apart: 2 -> 0, of which waited for: 2 -> 0; matrix products, arithmetic and copies ran while one was open for 1% -> 0% of each run, Pallas kernels for 0% -> 0%
where the time goes in v1:
time: 239 us; the launch traced here: 236 us
  Pallas kernels  217 us (91%)
  local copies, waits for them, and re-layouts  8.61 us (4%)
  blocking collectives  7.89 us (3%)
    pallas_call x1, Pallas kernels, shards(): pl.pallas_call(functools.partial(scatter_kernel, n, strips, blocks, cs),...  110 us
    pallas_call x1, Pallas kernels, shards(): pl.pallas_call(functools.partial(refer_kernel, n, strips, blocks, cs, die...  95.8 us
    pallas_call x1, Pallas kernels, shards(): pl.pallas_call(functools.partial(residual_kernel, strips, blocks, cs), na...  11.6 us
    unnamed x1, blocking collectives  7.89 us
    unnamed x8, local copies, waits for them, and re-layouts  7.67 us

profile of v1, /device:TPU:13, one launch (start us, length us, event | category | flops | bytes accessed | tf_op | source)
XLA Modules:
  0.0 235.9 jit_solution(10815527415434266163)
XLA Ops:
  0.0 1.2 dynamic-slice
  1.9 0.8 reshape.14.kern
  2.7 0.8 add_dynamic-update-slice_fusion
  3.4 7.9 %all-reduce = s32[256]{0:T(256)S(1)} all-reduce(s32[256]{0:T(256)S(1)} %add_dynamic-update-slice_fusion), channel_id=1, replica_groups=mesh['wafer'=2,'die'=16] {'die'}, use_global_device_ids=true, to_apply=%add | all-reduce | flops 256 | bytes 2048
  11.3 0.1 select_reduce_fusion.where
  11.4 0.7 convert_bitcast_fusion
  12.1 0.1 copy.8
  12.2 0.1 reshape.13.live
  12.3 109.8 %scatter.1 = (f32[16,16,8,512]{3,2,1,0:T(8,128)}, f32[16,2,8,512]{3,2,1,0:T(8,128)}) custom-call(f32[16,64,1024]{2,1,0:T(8,128)} %tile.1, f32[2,64,1024]{2,1,0:T(8,128)} %strength.1), custom_call_target="tpu_custom_call" | custom-call | tf_op jit(solution)/shard_map/scatter/pallas_call | solution.py:247
  122.0 0.0 copy-start.1
  122.1 2.2 copy-done.1
  124.2 0.0 copy-start.2
  124.2 1.0 copy-done.2
  125.3 95.8 %refer.1 = f32[8,2,32,8,512]{4,3,2,1,0:T(8,128)S(1)} custom-call(s32[256]{0:T(256)S(1)} %select_reduce_fusion.where, f32[256]{0:T(256)S(1)} %reshape.13.live, f32[25]{0:T(128)S(1)} %reshape.14.kern, f32[256,8,512]{2,1,0:T(8,128)S(1)} %bitcast.5, f32[32,8,512]{2,1,0:T(8,128)S(1)} %bitcast.6), custom_call_target="tpu_custom_call" | custom-call | tf_op jit(solution)/shard_map/refer/pallas_call | solution.py:262
  221.1 0.0 copy-start
  221.1 3.2 %copy-done = f32[8,2,32,8,512]{4,3,2,1,0:T(8,128)} copy-done((f32[8,2,32,8,512]{4,3,2,1,0:T(8,128)}, f32[8,2,32,8,512]{4,3,2,1,0:T(8,128)S(1)}, u32[]{:S(2)}) %copy-start) | copy-done | bytes 8388632
  224.3 11.6 %residual.1 = f32[16,64,1024]{2,1,0:T(8,128)} custom-call(s32[16]{0:T(128)} %pos.1, s32[16]{0:T(128)} %die.1, s32[8,32]{1,0:T(8,128)} %present.1, f32[16,64,1024]{2,1,0:T(8,128)} %tile.1, f32[8,2,32,8,512]{4,3,2,1,0:T(8,128)} %copy-done), custom_call_target="tpu_custom_call" | custom-call | tf_op jit(solution)/shard_map/residual/pallas_call | solution.py:301
  (1 shorter events, 0.0 us)
Async XLA Ops:
  122.0 2.2 copy-start.1
  124.2 1.0 copy-start.2
  221.1 3.2 %copy-start = (f32[8,2,32,8,512]{4,3,2,1,0:T(8,128)}, f32[8,2,32,8,512]{4,3,2,1,0:T(8,128)S(1)}, u32[]{:S(2)}) copy-start(f32[8,2,32,8,512]{4,3,2,1,0:T(8,128)S(1)} %refer.1) | copy-start | bytes 25165828

commit v2 on v1

--- a/solution.py
+++ b/solution.py
@@ -10,6 +10,7 @@
 ITERS = 3
 RS = 8
 LANES = 128
+PARTS = 4
 
 
 def strip_of(q, strips):
@@ -38,42 +39,17 @@
     )
 
 
-def scatter_kernel(n, strips, blocks, cs, tiles, strength, arrived, power, send, recv, psend, precv, own):
-    me = lax.axis_index("die")
-
-    def region(device):
-        s = strip_of(device // blocks, strips)
-        c = device % blocks
-        return pl.ds(pl.multiple_of(s * RS, RS), RS), pl.ds(pl.multiple_of(c * cs, LANES), cs)
-
-    greet(n)
-    copies = []
-    for k in range(1, n):
-        peer = (me + k) % n
-        rows, cols = region(peer)
-        copies.append(remote(tiles.at[:, rows, cols], arrived.at[me], send.at[k], recv.at[k], peer))
-        copies[-1].start()
-    for k in range(1, n):
-        peer = (me + k) % n
-        rows, cols = region(peer)
-        copies.append(remote(strength.at[:, rows, cols], power.at[me], psend.at[k], precv.at[k], peer))
-        copies[-1].start()
-    rows, cols = region(me)
-    copies.append(pltpu.make_async_copy(tiles.at[:, rows, cols], arrived.at[me], own.at[0]))
-    copies[-1].start()
-    copies.append(pltpu.make_async_copy(strength.at[:, rows, cols], power.at[me], own.at[1]))
-    copies[-1].start()
-    for copy in copies:
-        copy.wait()
-
-
 def refer_kernel(
     n, strips, blocks, cs, dies, positions,
-    where, live, kern, arrived, power, out,
-    stack, strength, mean, top, bottom, rows_up, rows_down, side_left, side_right, corners, ext, refer,
-    load, hsend, hrecv, rsend, rrecv, ssend, srecv, own,
+    live, kern, pair, tiles, power, out,
+    stacks, strength, pairs, table, where, mean,
+    top, bottom, rows_up, rows_down, side_left, side_right, corners, ext, refer,
+    send, recv, psend, precv, qsend, qrecv, local, hsend, hrecv, rsend, rrecv, ssend, srecv, own,
 ):
     me = lax.axis_index("die")
+    slots = tiles.shape[0]
+    held = power.shape[0]
+    chunks = cs // LANES
     s = strip_of(me // blocks, strips)
     c = me % blocks
     groups = positions // 4
@@ -81,15 +57,69 @@
     def device(ds, dc):
         return chip_of((s + ds + strips) % strips, strips) * blocks + (c + dc + blocks) % blocks
 
-    loads = [
-        pltpu.make_async_copy(arrived, stack, load.at[0]),
-        pltpu.make_async_copy(power, strength, load.at[1]),
+    def rows_of(peer):
+        return pl.ds(pl.multiple_of(strip_of(peer // blocks, strips) * RS, RS), RS)
+
+    def cols_of(peer, start, size):
+        return pl.ds(pl.multiple_of((peer % blocks) * cs + start, LANES), size)
+
+    tile_rows = pl.ds(me * slots, slots)
+    power_rows = pl.ds(me * held, held)
+    greet(n)
+    pair_copies = [pltpu.make_async_copy(pair, pairs.at[tile_rows], local.at[0])]
+    for k in range(1, n):
+        pair_copies.append(remote(pair, pairs.at[tile_rows], qsend.at[k], qrecv.at[k], (me + k) % n))
+    for copy in pair_copies:
+        copy.start()
+    tile_copies = []
+    for u in range(chunks):
+        wave = [
+            pltpu.make_async_copy(
+                tiles.at[:, rows_of(me), cols_of(me, u * LANES, LANES)], stacks[u].at[tile_rows], local.at[2 + u]
+            )
+        ]
+        for k in range(1, n):
+            peer = (me + k) % n
+            wave.append(
+                remote(
+                    tiles.at[:, rows_of(peer), cols_of(peer, u * LANES, LANES)], stacks[u].at[tile_rows],
+                    send.at[u, k], recv.at[u, k], peer,
+                )
+            )
+        for copy in wave:
+            copy.start()
+        tile_copies.append(wave)
+    power_copies = [
+        pltpu.make_async_copy(power.at[:, rows_of(me), cols_of(me, 0, cs)], strength.at[power_rows], local.at[1])
     ]
-    for copy in loads:
+    for k in range(1, n):
+        peer = (me + k) % n
+        power_copies.append(
+            remote(
+                power.at[:, rows_of(peer), cols_of(peer, 0, cs)], strength.at[power_rows],
+                psend.at[k], precv.at[k], peer,
+            )
+        )
+    for copy in power_copies:
         copy.start()
-    greet(n)
-    for copy in loads:
+
+    for copy in pair_copies:
         copy.wait()
+    order = lax.broadcasted_iota(jnp.int32, (n * slots, LANES), 0)
+    target = lax.broadcasted_iota(jnp.int32, (n * slots, LANES), 1)
+    for w in range(table.shape[0]):
+        hit = pairs[...] == target + w * LANES
+        table[w : w + 1, :] = jnp.max(jnp.where(hit, order, 0), axis=0, keepdims=True)
+    fetch = pltpu.make_async_copy(table, where, local.at[2 + chunks])
+    fetch.start()
+    fetch.wait()
+
+    def value_of(p, d, some):
+        q = p * dies + d
+        entry = where[q // LANES, q % LANES]
+        if len(some) == 1:
+            return stacks[some[0]][entry]
+        return jnp.concatenate([stacks[u][entry] for u in some], axis=1)
 
     first = pl.ds(0, LANES)
     last = pl.ds(cs - LANES, LANES)
@@ -150,71 +180,97 @@
         power_p = strength[p]
         return (field + power_p * acc) / (1.0 + power_p * total)
 
-    def huber(k, g, j, ref):
+    def huber(k, g, j, ref, some):
+        lanes = pl.ds(some[0] * LANES, len(some) * LANES)
         p = 4 * g + j
         num = None
         for d in range(dies):
-            value = stack[where[p * dies + d]]
+            value = value_of(p, d, some)
             weight = live[p * dies + d] / jnp.maximum(jnp.abs(value - ref), 1.5)
             num, den = (weight * value, weight) if num is None else (num + weight * value, den + weight)
         field = num / den
-        mean[k, p] = field
-        top[k, g, 2 * j : 2 * j + 2, :] = field[0:2]
-        bottom[k, g, 2 * j : 2 * j + 2, :] = field[RS - 2 : RS]
-
-    @pl.loop(0, groups)
-    def _(g):
-        for j in range(4):
-            p = 4 * g + j
-            count = live[p * dies]
-            num = count * stack[where[p * dies]]
-            for d in range(1, dies):
-                share = live[p * dies + d]
-                count = count + share
-                num = num + share * stack[where[p * dies + d]]
-            huber(0, g, j, num / jnp.full(num.shape, count))
-
-    for k in range(1, ITERS):
-        exchange(k - 1)
+        mean[k, p, :, lanes] = field
+        top[k, g, 2 * j : 2 * j + 2, lanes] = field[0:2]
+        bottom[k, g, 2 * j : 2 * j + 2, lanes] = field[RS - 2 : RS]
+
+    for u in range(chunks):
+        some = (u,)
+        for copy in tile_copies[u]:
+            copy.wait()
 
         @pl.loop(0, groups)
         def _(g):
             for j in range(4):
-                huber(k, g, j, smooth(k - 1, g, j))
+                p = 4 * g + j
+                count = live[p * dies]
+                num = count * value_of(p, 0, some)
+                for d in range(1, dies):
+                    share = live[p * dies + d]
+                    count = count + share
+                    num = num + share * value_of(p, d, some)
+                huber(0, g, j, num / jnp.full(num.shape, count), some)
+
+    for copy in power_copies:
+        copy.wait()
+
+    for k in range(1, ITERS):
+        exchange(k - 1)
+
+        @pl.loop(0, groups)
+        def _(g):
+            for j in range(4):
+                huber(k, g, j, smooth(k - 1, g, j), tuple(range(chunks)))
 
     exchange(ITERS - 1)
-
-    @pl.loop(0, groups)
-    def _(g):
-        for j in range(4):
-            refer[4 * g + j] = smooth(ITERS - 1, g, j)
 
     turn = 1 - 2 * (c % 2)
     ahead = device(turn, 0)
-    mine = pltpu.make_async_copy(refer, out.at[s, c], own)
-    mine.start()
+    parts = rsend.shape[1]
+    span = positions // parts
     pending = []
-    for t in range(strips):
+    rings = {}
+    mine = []
+
+    def forward(t, h):
         strip = (s - turn * t + strips) % strips
-        block = refer if t == 0 else out.at[strip, c]
+        part = pl.ds(h * span, span)
+        target = out.at[strip, c, part]
+        block = target if t else refer.at[part]
         if t:
-            ring.wait_recv()
+            rings[t - 1, h].wait_recv()
+        copies = [remote(block, target, ssend.at[t, h, b], srecv.at[t, h, b], device(0, b)) for b in range(1, blocks)]
         if t < strips - 1:
-            ring = remote(block, out.at[strip, c], rsend.at[t], rrecv.at[t], ahead)
-            ring.start()
-            pending.append(ring)
-        for b in range(1, blocks):
-            side = remote(block, out.at[strip, c], ssend.at[t, b], srecv.at[t, b], device(0, b))
-            side.start()
-            pending.append(side)
+            rings[t, h] = remote(block, target, rsend.at[t, h], rrecv.at[t, h], ahead)
+            copies.insert(0, rings[t, h])
+        for copy in copies:
+            copy.start()
+        pending.extend(copies)
+
+    for h in range(parts):
+
+        @pl.loop(h * span // 4, (h + 1) * span // 4)
+        def _(g):
+            for j in range(4):
+                refer[4 * g + j] = smooth(ITERS - 1, g, j)
+
+        part = pl.ds(h * span, span)
+        mine.append(pltpu.make_async_copy(refer.at[part], out.at[s, c, part], own.at[h]))
+        mine[-1].start()
+        forward(0, h)
+    for t in range(1, strips):
+        for h in range(parts):
+            forward(t, h)
     for copy in pending:
         copy.wait_send()
     for t in range(strips):
-        for b in range(1, blocks):
-            source = (c - b + blocks) % blocks
-            strip = (s - (1 - 2 * (source % 2)) * t + strips) % strips
-            remote(out.at[strip, source], out.at[strip, source], ssend.at[t, b], srecv.at[t, b], device(0, b)).wait_recv()
-    mine.wait()
+        for h in range(parts):
+            for b in range(1, blocks):
+                source = (c - b + blocks) % blocks
+                strip = (s - (1 - 2 * (source % 2)) * t + strips) % strips
+                target = out.at[strip, source, pl.ds(h * span, span)]
+                remote(target, target, ssend.at[t, h, b], srecv.at[t, h, b], device(0, b)).wait_recv()
+    for copy in mine:
+        copy.wait()
 
 
 def residual_kernel(strips, blocks, cs, pos, die, present, tile, refer, out):
@@ -229,7 +285,6 @@
 def shards(n, die_tiles, slot_pos, slot_die, present, strength, kernel):
     slots, rows, cols = die_tiles.shape
     dies, positions = present.shape
-    local = strength.shape[0]
     strips = rows // RS
     blocks = n // strips
     cs = cols // blocks
@@ -238,36 +293,23 @@
     dma = pltpu.SemaphoreType.DMA
     f32 = jnp.float32
 
-    pair = slot_pos * dies + slot_die
-    pairs = lax.all_gather(pair, "die", axis=0, tiled=True)
     count = positions * dies
-    order = jnp.arange(n * slots, dtype=jnp.int32)
-    where = jnp.sum(jnp.where(pairs[None, :] == jnp.arange(count, dtype=jnp.int32)[:, None], order[None, :], 0), axis=1)
-
-    arrived, power = pl.pallas_call(
-        functools.partial(scatter_kernel, n, strips, blocks, cs),
-        name="scatter",
-        out_shape=(
-            jax.ShapeDtypeStruct((n, slots, RS, cs), f32),
-            jax.ShapeDtypeStruct((n, local, RS, cs), f32),
-        ),
-        in_specs=[hbm, hbm],
-        out_specs=(hbm, hbm),
-        scratch_shapes=[dma((n,)), dma((n,)), dma((n,)), dma((n,)), dma((2,))],
-        compiler_params=pltpu.CompilerParams(collective_id=0, has_side_effects=True),
-    )(die_tiles, strength)
-
+    chunks = cs // LANES
+    pair = jnp.broadcast_to((slot_pos * dies + slot_die)[:, None], (slots, LANES))
     groups = positions // 4
     vmem = pltpu.VMEM
     refer = pl.pallas_call(
         functools.partial(refer_kernel, n, strips, blocks, cs, dies, positions),
         name="refer",
         out_shape=jax.ShapeDtypeStruct((strips, blocks, positions, RS, cs), f32),
-        in_specs=[smem, smem, smem, hbm, hbm],
+        in_specs=[smem, smem, pl.BlockSpec(memory_space=pltpu.VMEM), hbm, hbm],
         out_specs=hbm,
         scratch_shapes=[
-            vmem((n * slots, RS, cs), f32),
+            tuple(vmem((n * slots, RS, LANES), f32) for _ in range(chunks)),
             vmem((positions, RS, cs), f32),
+            vmem((n * slots, LANES), jnp.int32),
+            vmem((count // LANES, LANES), jnp.int32),
+            pltpu.SMEM((count // LANES, LANES), jnp.int32),
             vmem((ITERS, positions, RS, cs), f32),
             vmem((ITERS, groups, 8, cs), f32),
             vmem((ITERS, groups, 8, cs), f32),
@@ -278,24 +320,30 @@
             vmem((ITERS, 4, groups, 8, LANES), f32),
             vmem((4, 24, cs + 2 * LANES), f32),
             vmem((positions, RS, cs), f32),
-            dma((2,)),
+            dma((chunks, n)),
+            dma((chunks, n)),
+            dma((n,)),
+            dma((n,)),
+            dma((n,)),
+            dma((n,)),
+            dma((3 + chunks,)),
             dma((ITERS, 8)),
             dma((ITERS, 8)),
-            dma((strips,)),
-            dma((strips,)),
-            dma((strips, blocks)),
-            dma((strips, blocks)),
-            dma,
+            dma((strips, PARTS)),
+            dma((strips, PARTS)),
+            dma((strips, PARTS, blocks)),
+            dma((strips, PARTS, blocks)),
+            dma((PARTS,)),
         ],
         compiler_params=pltpu.CompilerParams(
-            collective_id=1, has_side_effects=True, vmem_limit_bytes=40 * 1024 * 1024
+            collective_id=0, has_side_effects=True, vmem_limit_bytes=40 * 1024 * 1024
         ),
     )(
-        where,
         present.T.astype(f32).reshape(count),
         kernel.reshape(25),
-        arrived.reshape(n * slots, RS, cs),
-        power.reshape(positions, RS, cs),
+        pair,
+        die_tiles,
+        strength,
     )
 
     return pl.pallas_call(

time: 239 us -> 210 us (0.88)
  Pallas kernels: 217 us -> 199 us
  blocking collectives: 7.89 us -> 0 us
    pallas_call x1 -> x0, Pallas kernels: 110 us -> none  [shards(): pl.pallas_call(functools.partial(scatter_kernel, n, strips, blocks, cs),...]
    pallas_call x1, Pallas kernels: 95.8 us -> 187 us  [shards(): pl.pallas_call(functools.partial(refer_kernel, n, strips, blocks, cs, die...]
    unnamed x1 -> x0, blocking collectives: 7.89 us -> none
    unnamed x8 -> x6, local copies, waits for them, and re-layouts: 7.67 us -> 6.44 us
where the time goes in v2:
time: 210 us; the launch traced here: 208 us
  Pallas kernels  199 us (95%)
  local copies, waits for them, and re-layouts  7.44 us (4%)
    pallas_call x1, Pallas kernels, shards(): pl.pallas_call(functools.partial(refer_kernel, n, strips, blocks, cs, die...  187 us
    pallas_call x1, Pallas kernels, shards(): pl.pallas_call(functools.partial(residual_kernel, strips, blocks, cs), na...  11.6 us
    unnamed x6, local copies, waits for them, and re-layouts  6.44 us

profile of v2, /device:TPU:13, one launch (start us, length us, event | category | flops | bytes accessed | tf_op | source)
XLA Modules:
  0.0 207.5 jit_solution(7787800135992097101)
XLA Ops:
  0.0 0.8 reshape.8.kern
  0.8 0.7 multiply_add_fusion
  1.4 0.7 convert_bitcast_fusion
  2.1 0.1 broadcast_in_dim.2.pair
  2.2 0.1 copy.7
  2.3 0.1 reshape.7.live
  2.4 0.0 copy-start.1
  2.4 2.2 %copy-done.1 = f32[16,64,1024]{2,1,0:T(8,128)S(1)} copy-done((f32[16,64,1024]{2,1,0:T(8,128)S(1)}, f32[16,64,1024]{2,1,0:T(8,128)}, u32[]{:S(2)}) %copy-start.1) | copy-done | bytes 4194328
  4.6 0.0 copy-start.2
  4.6 1.0 copy-done.2
  5.6 187.1 %refer.1 = f32[8,2,32,8,512]{4,3,2,1,0:T(8,128)S(1)} custom-call(f32[256]{0:T(256)S(1)} %reshape.7.live, f32[25]{0:T(128)S(1)} %reshape.8.kern, s32[16,128]{1,0:T(8,128)S(1)} %broadcast_in_dim.2.pair, f32[16,64,1024]{2,1,0:T(8,128)S(1)} %copy-done.1, f32[2,64,1024]{2,1,0:T(8,128)S(1)} %copy-done.2), custom_call_target="tpu_custom_call" | custom-call | tf_op jit(solution)/shard_map/refer/pallas_call | solution.py:301
  192.7 0.0 copy-start
  192.7 3.2 %copy-done = f32[8,2,32,8,512]{4,3,2,1,0:T(8,128)} copy-done((f32[8,2,32,8,512]{4,3,2,1,0:T(8,128)}, f32[8,2,32,8,512]{4,3,2,1,0:T(8,128)S(1)}, u32[]{:S(2)}) %copy-start) | copy-done | bytes 8388632
  195.9 11.6 %residual.1 = f32[16,64,1024]{2,1,0:T(8,128)} custom-call(s32[16]{0:T(128)} %pos.1, s32[16]{0:T(128)} %die.1, s32[8,32]{1,0:T(8,128)} %present.1, f32[16,64,1024]{2,1,0:T(8,128)} %tile.1, f32[8,2,32,8,512]{4,3,2,1,0:T(8,128)} %copy-done), custom_call_target="tpu_custom_call" | custom-call | tf_op jit(solution)/shard_map/residual/pallas_call | solution.py:349
Async XLA Ops:
  2.4 2.2 %copy-start.1 = (f32[16,64,1024]{2,1,0:T(8,128)S(1)}, f32[16,64,1024]{2,1,0:T(8,128)}, u32[]{:S(2)}) copy-start(f32[16,64,1024]{2,1,0:T(8,128)} %tile.1) | copy-start | bytes 12582916
  4.6 1.0 copy-start.2
  192.7 3.2 %copy-start = (f32[8,2,32,8,512]{4,3,2,1,0:T(8,128)}, f32[8,2,32,8,512]{4,3,2,1,0:T(8,128)S(1)}, u32[]{:S(2)}) copy-start(f32[8,2,32,8,512]{4,3,2,1,0:T(8,128)S(1)} %refer.1) | copy-start | bytes 25165828

commit v3 on v2

--- a/solution.py
+++ b/solution.py
@@ -11,6 +11,8 @@
 RS = 8
 LANES = 128
 PARTS = 4
+HALVES = 2
+PER_STEP = 2
 
 
 def strip_of(q, strips):
@@ -130,21 +132,27 @@
             if a or b:
                 total = total + taps[a][b]
 
-    def exchange(k):
+    def exchange(k, h):
+        size = groups // HALVES
+        g = pl.ds(h * size, size)
+        p = pl.ds(h * size * 4, size * 4)
+        moves = [
+            (bottom.at[k, g], rows_up.at[k, g], 1, 0),
+            (top.at[k, g], rows_down.at[k, g], -1, 0),
+            (mean.at[k, p, :, last], side_left.at[k, p], 0, 1),
+            (mean.at[k, p, :, first], side_right.at[k, p], 0, -1),
+            (bottom.at[k, g, :, last], corners.at[k, 0, g], 1, 1),
+            (bottom.at[k, g, :, first], corners.at[k, 1, g], 1, -1),
+            (top.at[k, g, :, last], corners.at[k, 2, g], -1, 1),
+            (top.at[k, g, :, first], corners.at[k, 3, g], -1, -1),
+        ]
         copies = [
-            remote(bottom.at[k], rows_up.at[k], hsend.at[k, 0], hrecv.at[k, 0], device(1, 0)),
-            remote(top.at[k], rows_down.at[k], hsend.at[k, 1], hrecv.at[k, 1], device(-1, 0)),
-            remote(mean.at[k, :, :, last], side_left.at[k], hsend.at[k, 2], hrecv.at[k, 2], device(0, 1)),
-            remote(mean.at[k, :, :, first], side_right.at[k], hsend.at[k, 3], hrecv.at[k, 3], device(0, -1)),
-            remote(bottom.at[k, :, :, last], corners.at[k, 0], hsend.at[k, 4], hrecv.at[k, 4], device(1, 1)),
-            remote(bottom.at[k, :, :, first], corners.at[k, 1], hsend.at[k, 5], hrecv.at[k, 5], device(1, -1)),
-            remote(top.at[k, :, :, last], corners.at[k, 2], hsend.at[k, 6], hrecv.at[k, 6], device(-1, 1)),
-            remote(top.at[k, :, :, first], corners.at[k, 3], hsend.at[k, 7], hrecv.at[k, 7], device(-1, -1)),
+            remote(src, dst, hsend.at[k, h, m], hrecv.at[k, h, m], device(ds, dc))
+            for m, (src, dst, ds, dc) in enumerate(moves)
         ]
         for copy in copies:
             copy.start()
-        for copy in copies:
-            copy.wait()
+        return copies
 
     def guard(flag, x):
         return jnp.where(flag, x, jnp.zeros_like(x))
@@ -210,18 +218,22 @@
                     num = num + share * value_of(p, d, some)
                 huber(0, g, j, num / jnp.full(num.shape, count), some)
 
+    halo = [exchange(0, h) for h in range(HALVES)]
     for copy in power_copies:
         copy.wait()
-
     for k in range(1, ITERS):
-        exchange(k - 1)
-
-        @pl.loop(0, groups)
-        def _(g):
-            for j in range(4):
-                huber(k, g, j, smooth(k - 1, g, j), tuple(range(chunks)))
-
-    exchange(ITERS - 1)
+        later = []
+        for h in range(HALVES):
+            for copy in halo[h]:
+                copy.wait()
+
+            @pl.loop(h * groups // HALVES, (h + 1) * groups // HALVES)
+            def _(g):
+                for j in range(4):
+                    huber(k, g, j, smooth(k - 1, g, j), tuple(range(chunks)))
+
+            later.append(exchange(k, h))
+        halo = later
 
     turn = 1 - 2 * (c % 2)
     ahead = device(turn, 0)
@@ -247,6 +259,9 @@
         pending.extend(copies)
 
     for h in range(parts):
+        if h * HALVES % parts == 0:
+            for copy in halo[h * HALVES // parts]:
+                copy.wait()
 
         @pl.loop(h * span // 4, (h + 1) * span // 4)
         def _(g):
@@ -273,13 +288,19 @@
         copy.wait()
 
 
-def residual_kernel(strips, blocks, cs, pos, die, present, tile, refer, out):
-    i = pl.program_id(0)
-    keep = present[die[i], pos[i]].astype(jnp.float32)
-    for s in range(strips):
-        for c in range(blocks):
-            rows, cols = pl.ds(s * RS, RS), pl.ds(c * cs, cs)
-            out[0, rows, cols] = keep * (tile[0, rows, cols] - refer[s, c, 0])
+def residual_kernel(strips, blocks, cs, pos, die, present, tile, *rest):
+    out = rest[-1]
+    for u in range(PER_STEP):
+        slot = pl.program_id(0) * PER_STEP + u
+        keep = present[die[slot], pos[slot]].astype(jnp.float32)
+        for s in range(strips):
+            for c in range(blocks):
+                rows, cols = pl.ds(s * RS, RS), pl.ds(c * cs, cs)
+                out[u, rows, cols] = keep * (tile[u, rows, cols] - rest[u][s, c, 0])
+
+
+def refer_spec(strips, blocks, cs, u):
+    return pl.BlockSpec((strips, blocks, 1, RS, cs), lambda i, pos, *_: (0, 0, pos[i * PER_STEP + u], 0, 0))
 
 
 def shards(n, die_tiles, slot_pos, slot_die, present, strength, kernel):
@@ -288,7 +309,7 @@
     strips = rows // RS
     blocks = n // strips
     cs = cols // blocks
-    hbm = pl.BlockSpec(memory_space=pl.ANY)
+    hbm = pl.BlockSpec(memory_space=pltpu.HBM)
     smem = pl.BlockSpec(memory_space=pltpu.SMEM)
     dma = pltpu.SemaphoreType.DMA
     f32 = jnp.float32
@@ -327,8 +348,8 @@
             dma((n,)),
             dma((n,)),
             dma((3 + chunks,)),
-            dma((ITERS, 8)),
-            dma((ITERS, 8)),
+            dma((ITERS, HALVES, 8)),
+            dma((ITERS, HALVES, 8)),
             dma((strips, PARTS)),
             dma((strips, PARTS)),
             dma((strips, PARTS, blocks)),
@@ -336,7 +357,7 @@
             dma((PARTS,)),
         ],
         compiler_params=pltpu.CompilerParams(
-            collective_id=0, has_side_effects=True, vmem_limit_bytes=40 * 1024 * 1024
+            collective_id=0, has_side_effects=True, vmem_limit_bytes=56 * 1024 * 1024
         ),
     )(
         present.T.astype(f32).reshape(count),
@@ -352,14 +373,15 @@
         out_shape=jax.ShapeDtypeStruct((slots, rows, cols), f32),
         grid_spec=pltpu.PrefetchScalarGridSpec(
             num_scalar_prefetch=3,
-            grid=(slots,),
+            grid=(slots // PER_STEP,),
             in_specs=[
-                pl.BlockSpec((1, rows, cols), lambda i, *_: (i, 0, 0)),
-                pl.BlockSpec((strips, blocks, 1, RS, cs), lambda i, pos, *_: (0, 0, pos[i], 0, 0)),
+                pl.BlockSpec((PER_STEP, rows, cols), lambda i, *_: (i, 0, 0)),
+                *[refer_spec(strips, blocks, cs, u) for u in range(PER_STEP)],
             ],
-            out_specs=pl.BlockSpec((1, rows, cols), lambda i, *_: (i, 0, 0)),
+            out_specs=pl.BlockSpec((PER_STEP, rows, cols), lambda i, *_: (i, 0, 0)),
         ),
-    )(slot_pos, slot_die, present, die_tiles, refer)
+        compiler_params=pltpu.CompilerParams(vmem_limit_bytes=56 * 1024 * 1024),
+    )(slot_pos, slot_die, present, die_tiles, *[refer] * PER_STEP)
 
 
 def solution(mesh):

time: 210 us -> 189 us (0.900)
  Pallas kernels: 199 us -> 183 us
  local copies, waits for them, and re-layouts: 7.44 us -> 2.64 us
    pallas_call x1, Pallas kernels: 187 us -> 174 us  [shards(): pl.pallas_call(functools.partial(refer_kernel, n, strips, blocks, cs, die...]
    unnamed x6 -> x0, local copies, waits for them, and re-layouts: 6.44 us -> none
    pallas_call x1, Pallas kernels: 11.6 us -> 8.33 us  [shards(): pl.pallas_call(functools.partial(residual_kernel, strips, blocks, cs), na...]
where the time goes in v3:
time: 189 us; the launch traced here: 187 us
  Pallas kernels  183 us (97%)
  local copies, waits for them, and re-layouts  2.64 us (1%)
    pallas_call x1, Pallas kernels, shards(): pl.pallas_call(functools.partial(refer_kernel, n, strips, blocks, cs, die...  174 us
    pallas_call x1, Pallas kernels, shards(): pl.pallas_call(functools.partial(residual_kernel, strips, blocks, cs), na...  8.33 us

profile of v3, /device:TPU:13, one launch (start us, length us, event | category | flops | bytes accessed | tf_op | source)
XLA Modules:
  0.0 186.7 jit_solution(15672648719340071278)
XLA Ops:
  0.0 1.3 reshape.8.kern
  1.3 0.7 multiply_add_fusion
  2.0 0.7 convert_bitcast_fusion
  2.7 0.7 broadcast_in_dim.2.pair
  3.3 0.1 copy.7
  3.4 0.6 reshape.7.live
  4.0 174.4 %refer.1.rest_0_.rest_1_ = f32[8,2,32,8,512]{4,3,2,1,0:T(8,128)} custom-call(f32[256]{0:T(256)} %reshape.7.live, f32[25]{0:T(128)} %reshape.8.kern, s32[16,128]{1,0:T(8,128)} %broadcast_in_dim.2.pair, f32[16,64,1024]{2,1,0:T(8,128)} %tile.1, f32[2,64,1024]{2,1,0:T(8,128)} %power.1), custom_call_target="tpu_custom_call" | custom-call | tf_op jit(solution)/shard_map/refer/pallas_call | solution.py:322
  178.4 8.3 %residual.1 = f32[16,64,1024]{2,1,0:T(8,128)} custom-call(s32[16]{0:T(128)} %pos.1, s32[16]{0:T(128)} %die.1, s32[8,32]{1,0:T(8,128)} %present.1, f32[16,64,1024]{2,1,0:T(8,128)} %tile.1, f32[8,2,32,8,512]{4,3,2,1,0:T(8,128)} %refer.1.rest_0_.rest_1_, f32[8,2,32,8,512]{4,3,2,1,0:T(8,128)} %refer.1.rest_0_.rest_1_), custom_call_target="tpu_custom_call" | custom-call | tf_op jit(solution)/shard_map/residual/pallas_call | solution.py:370
